TPU v7x, 256 devices: a whole 4x4x8 slice. The times are simulated.
256 devices in a mesh: lat: 16 (over x, y), lon: 8 (over z), ens: 2 (over core).
Axes of the slice: x: 4, y: 4, z: 8, core: 2. Of those that a mesh axis runs over, the one named last changes fastest.
Arguments:
- parameters: float32 [2, 128, 128, 1024], P(None, 'ens', 'lat', 'lon'), may hold values from -1.2 to 1.2, as said below
- initial_height: float32 [128, 1024], P('lat', 'lon'), may hold values from -6 to 6
- initial_speed: float32 [2, 128, 1024], P(None, 'lat', 'lon'), may hold values from -4 to 4
- obs_slots: int32 [2, 128, 128, 8], P(None, ('lat', 'lon')), may hold values from -1 to 1023, as said below
- obs_values: float32 [2, 128, 128, 8], P(None, ('lat', 'lon')), may hold values from -6 to 6
- obs_precision: float32 [2, 128, 128, 8], P(None, ('lat', 'lon')), may hold values from 0 to 2, as said below
Outputs:
- calibrated: float32 [2, 128, 128, 1024], P(None, 'ens', 'lat', 'lon')
Inputs may be any that keep to these rules, and one draw needn't show every extreme that they name: `obs_slots`: for each iteration and owner, the live slots towards one receiver come first and name distinct cells of the owner's block (local index row * 128 + column); no cell is named twice by one owner in one iteration; in each iteration some receiving block has all 8 slots live from every owner. `obs_precision`: zero exactly where the matching slot of obs_slots (with receiver and owner swapped) is empty, 0.5 or more elsewhere. `parameters`: friction rates lie in 0.02 to 0.2, forcing in -1.2 to 1.2.
All inputs are finite; a program needn't handle non-finite values.
Results may differ from a plain program's by a relative error of at most 0.0003.
Values sent between devices are 32-bit elements; how exact they have to be, the bound alone decides.
No kernel may reach another device: no remote copies, remote signals or barrier semaphores. Data moves between devices by JAX's collectives and lax.ppermute only.
A program may use at most 64 MiB of HBM per device.

v0:
```python
import math
import jax
import jax.numpy as jnp
from jax import lax
from jax.sharding import Mesh
from jax.sharding import PartitionSpec as P

STEPS = 6
ITERS = 2
LAT = ("lat_0", "lat_1")
LAT_LON = ("lat_0", "lat_1", "lon")
depth_step = 0.7
gravity_step = 0.7
coriolis = 0.1


def padded_2(value, sides, width, wrap):
    for axis, dim in sides:
        peers, length = (lax.axis_size(axis), value.shape[dim])
        up = [(i, (i + 1) % peers) for i in range(peers if wrap else peers - 1)]
        down = [(j, i) for i, j in up]
        last = lax.slice_in_dim(value, length - width, length, axis=dim)
        leading = lax.slice_in_dim(value, 0, width, axis=dim)
        before = lax.ppermute(last, axis, up)
        after = lax.ppermute(leading, axis, down)
        value = jnp.concatenate([before, value, after], axis=dim)
    return value


def with_halo(value, sides, width):
    edges = {}
    for axis, dim in sides:
        peers, length = (lax.axis_size(axis), value.shape[dim])
        up = [(i, (i + 1) % peers) for i in range(peers)]
        last = lax.slice_in_dim(value, length - width, length, axis=dim)
        leading = lax.slice_in_dim(value, 0, width, axis=dim)
        edges[dim] = (
            lax.ppermute(last, axis, up),
            lax.ppermute(leading, axis, [(b, a) for a, b in up]),
        )
    done = []
    for _, dim in sides:
        low, high = edges[dim]
        around = [(width, width) if d in done else (0, 0) for d in range(value.ndim)]
        value = jnp.concatenate([jnp.pad(low, around), value, jnp.pad(high, around)], axis=dim)
        done.append(dim)
    return value


def in_one_piece(arrays, axis, split_dim, concat_dim, along):
    widths = [a.shape[along] for a in arrays]
    both = jnp.concatenate(arrays, axis=along)
    result = lax.all_to_all(both, axis, split_axis=split_dim, concat_axis=concat_dim, tiled=True)
    return tuple(jnp.split(result, [sum(widths[:k]) for k in range(1, len(widths))], axis=along))


def one_axis_at_a_time(value, axes):
    for axis in axes:
        value = lax.psum(value, axis)
    return value


def wall_rows(padded):
    row_count = padded.shape[-2]
    position = lax.axis_index(LAT)
    last_block = lax.axis_size(LAT) - 1
    row_ids = lax.broadcasted_iota(jnp.int32, (row_count, 1), 0)
    lower_wall = jnp.logical_and(row_ids == 0, position == 0)
    upper_wall = jnp.logical_and(row_ids == row_count - 1, position == last_block)
    keep_rows = jnp.logical_not(jnp.logical_or(lower_wall, upper_wall))
    return padded * keep_rows.astype(padded.dtype)


def advance(height, speeds, friction, forcing):
    east_padded = padded_2(speeds[0], (("lon", 2),), 1, True)
    north_padded = padded_2(speeds[1], ((LAT, 1),), 1, False)
    east_diff = east_padded[:, :, 2:] - east_padded[:, :, :-2]
    north_diff = north_padded[:, 2:, :] - north_padded[:, :-2, :]
    height = height - depth_step * (east_diff + north_diff) + forcing
    padded_height = with_halo(height, ((LAT, 1), ("lon", 2)), 1)
    padded_height = wall_rows(padded_height)
    slope_east = padded_height[:, 1:-1, 2:] - padded_height[:, 1:-1, :-2]
    slope_north = padded_height[:, 2:, 1:-1] - padded_height[:, :-2, 1:-1]
    eastward = (1.0 - friction) * speeds[0] - gravity_step * slope_east + coriolis * speeds[1]
    northward = (1.0 - friction) * speeds[1] - gravity_step * slope_north - coriolis * speeds[0]
    return (height, jnp.stack([eastward, northward]))


def forward(parameters, initial_height, initial_speed):
    members = parameters.shape[1]
    height = jnp.broadcast_to(initial_height, (members,) + initial_height.shape)
    speeds = jnp.broadcast_to(initial_speed[:, None], (2, members) + initial_height.shape)
    for substep in range(STEPS):
        height, speeds = advance(height, speeds, parameters[0], parameters[1])
    return height


def predict(height, cells):
    flattened = height.reshape(height.shape[0], -1)
    wanted = cells.reshape(-1)
    picked = jnp.take(flattened, jnp.clip(wanted, 0, flattened.shape[1] - 1), axis=1)
    picked = jnp.where(wanted[None, :] >= 0, picked, jnp.float32(0.0))
    return picked.T.reshape(cells.shape[0], -1)


def gram_terms(predicted, observed, precision):
    members = predicted.shape[1]
    centre = jnp.mean(predicted, axis=1, keepdims=True)
    spread = predicted - centre
    weighted = spread * precision[:, None]
    misfit = observed[:, None] - predicted
    gram_part = jnp.dot(spread.T, weighted, precision=lax.Precision.HIGHEST) / members
    cross_part = jnp.dot(weighted.T, misfit, precision=lax.Precision.HIGHEST) / math.sqrt(members)
    return (gram_part, cross_part)


def solve_weights(gram_part, cross_part):
    members = gram_part.shape[0]
    system = jnp.eye(members, dtype=jnp.float32) + gram_part
    factor = jnp.linalg.cholesky(system)
    weights = jax.scipy.linalg.cho_solve((factor, True), cross_part) / math.sqrt(members)
    return weights - jnp.mean(weights, axis=0, keepdims=True)


def per_device(parameters, initial_height, initial_speed, obs_slots, obs_values, obs_precision):
    owners = obs_slots.shape[2]
    slot_count = obs_slots.shape[3]
    members_here = parameters.shape[1]
    member_block = lax.axis_index("ens")
    owner_values, owner_precision = in_one_piece(
        (obs_values[:, 0], obs_precision[:, 0]), LAT_LON, 1, 1, 0
    )
    for iteration in range(ITERS):
        height = forward(parameters, initial_height, initial_speed)
        outgoing = predict(height, obs_slots[iteration, 0])
        received = outgoing
        observed = owner_values[iteration]
        precision = owner_precision[iteration]
        received = received.reshape(owners, slot_count, members_here)
        gathered = lax.all_gather(received, "ens", axis=2, tiled=True)
        members = gathered.shape[2]
        gram_part, cross_part = gram_terms(
            gathered.reshape(-1, members), observed.reshape(-1), precision.reshape(-1)
        )
        gram_part, cross_part = (
            one_axis_at_a_time(gram_part, LAT_LON),
            one_axis_at_a_time(cross_part, LAT_LON),
        )
        centred = solve_weights(gram_part, cross_part)
        local_weights = lax.dynamic_slice_in_dim(
            centred, member_block * members_here, members_here, 1
        )
        starting = jnp.zeros(
            (2, members_here, parameters.shape[2] * parameters.shape[3]), jnp.float32
        )
        pieces = lax.all_gather(parameters, "ens", axis=1, tiled=True)
        stacked = pieces.reshape(pieces.shape[0], pieces.shape[1], -1)
        increment = starting + jnp.einsum(
            "pjc,jm->pmc", stacked, local_weights, precision=lax.Precision.HIGHEST
        )
        parameters = parameters + increment.reshape(parameters.shape)
    return parameters


def solution(mesh):
    torus = Mesh(
        mesh.devices.reshape(4, 4, mesh.shape["lon"], mesh.shape["ens"]),
        ("lat_0", "lat_1", "lon", "ens"),
    )
    in_specs = (
        P(None, "ens", LAT, "lon"),
        P(LAT, "lon"),
        P(None, LAT, "lon"),
        P(None, LAT_LON, None, None),
        P(None, LAT_LON, None, None),
        P(None, LAT_LON, None, None),
    )
    out_specs = P(None, "ens", LAT, "lon")
    return jax.shard_map(
        per_device, mesh=torus, in_specs=in_specs, out_specs=out_specs, check_vma=False
    )
```

profile of v0, /device:TPU:2, one launch (start us, length us, event | category | flops | bytes accessed | tf_op | source)
XLA Modules:
  0.0 758.7 jit_solution(8578512216387290652)
XLA Ops:
  8.4 5.9 collective-permute-start
  14.5 4.9 collective-permute-start.2
  39.1 6.0 collective-permute-start.10
  49.3 4.3 collective-permute-done.8
  80.1 5.1 collective-permute-done.16
  99.3 8.5 %all-to-all-start = ((f32[4,128,8]{2,0,1:T(4,128)}), f32[4,128,8]{2,0,1:T(4,128)S(1)}, u32[]{:S(2)}, u32[]{:S(2)}) async-start(f32[4,128,8]{2,0,1:T(4,128)} %copy.61), calls=%async_computation | async-start | bytes 524288 | tf_op jit(solution)/shard_map/all_to_all | solution.py:53
  112.8 4.5 collective-permute-start.26
  140.1 5.8 collective-permute-start.34
  148.5 5.4 collective-permute-done.35
  169.9 6.1 collective-permute-start.42
  178.5 5.6 collective-permute-done.43
  193.8 43.5 %all-reduce.43.cloned.1.call-done = (f32[128,128]{1,0:T(8,128)}, f32[128,128]{0,1:T(8,128)}) async-done(((f32[128,128]{1,0:T(8,128)}, f32[128,128]{0,1:T(8,128)}), (f32[128,128]{1,0:T(8,128)}, f32[128,128]{0,1:T(8,128)})) %all-reduce.43.cloned.1.call-update) | async-done | bytes 131088 | tf_op jit(solution)/shard_map/psum | solution.py:59
  237.4 50.5 %all-reduce.39.cloned.1.call-done = (f32[128,128]{1,0:T(8,128)}, f32[128,128]{0,1:T(8,128)}) async-done(((f32[128,128]{1,0:T(8,128)}, f32[128,128]{0,1:T(8,128)}), (f32[128,128]{1,0:T(8,128)}, f32[128,128]{0,1:T(8,128)})) %all-reduce.39.cloned.1.call-update) | async-done | bytes 131088 | tf_op jit(solution)/shard_map/psum | solution.py:59
  288.5 74.1 %all-reduce.35.cloned.1.call-done = (f32[128,128]{1,0:T(8,128)}, f32[128,128]{0,1:T(8,128)}) async-done(((f32[128,128]{1,0:T(8,128)}, f32[128,128]{0,1:T(8,128)}), (f32[128,128]{1,0:T(8,128)}, f32[128,128]{0,1:T(8,128)})) %all-reduce.35.cloned.1.call-update) | async-done | bytes 131088 | tf_op jit(solution)/shard_map/psum | solution.py:59
  364.4 11.7 %cholesky.44 = f32[128,128]{1,0:T(8,128)S(1)} custom-call(f32[128,128]{1,0:T(8,128)S(1)} %fusion.178), custom_call_target="Cholesky" | custom-call | tf_op jit(solution)/shard_map/jit(cholesky)/cholesky | solution.py:120
  377.5 9.8 %custom-call.8 = f32[1,128,128]{1,2,0:T(8,128)S(1)} custom-call(f32[1,128,128]{2,1,0:T(8,128)S(1)} %fusion.163), custom_call_target="InvertDiagBlocksLowerTriangular" | custom-call | tf_op jit(solution)/shard_map/jit(_cho_solve)/triangular_solve | solution.py:121
  399.5 4.3 collective-permute-done.44
  418.2 4.5 collective-permute-done.49
  431.4 4.3 collective-permute-done.52
  448.2 4.3 collective-permute-done.56
  463.9 5.7 collective-permute-done.60
  479.0 4.3 collective-permute-done.64
  494.3 4.3 collective-permute-done.68
  499.8 4.5 collective-permute-start.74
  509.3 5.1 collective-permute-done.72
  530.3 6.0 collective-permute-start.82
  539.3 5.0 collective-permute-done.83
  552.9 43.8 %all-reduce.41.cloned.1.call-done = (f32[128,128]{1,0:T(8,128)}, f32[128,128]{0,1:T(8,128)}) async-done(((f32[128,128]{1,0:T(8,128)}, f32[128,128]{0,1:T(8,128)}), (f32[128,128]{1,0:T(8,128)}, f32[128,128]{0,1:T(8,128)})) %all-reduce.41.cloned.1.call-update) | async-done | bytes 131088 | tf_op jit(solution)/shard_map/psum | solution.py:59
  596.8 50.2 %all-reduce.37.cloned.1.call-done = (f32[128,128]{1,0:T(8,128)}, f32[128,128]{0,1:T(8,128)}) async-done(((f32[128,128]{1,0:T(8,128)}, f32[128,128]{0,1:T(8,128)}), (f32[128,128]{1,0:T(8,128)}, f32[128,128]{0,1:T(8,128)})) %all-reduce.37.cloned.1.call-update) | async-done | bytes 131088 | tf_op jit(solution)/shard_map/psum | solution.py:59
  647.6 74.1 %all-reduce.33.cloned.1.call-done = (f32[128,128]{1,0:T(8,128)}, f32[128,128]{0,1:T(8,128)}) async-done(((f32[128,128]{1,0:T(8,128)}, f32[128,128]{0,1:T(8,128)}), (f32[128,128]{1,0:T(8,128)}, f32[128,128]{0,1:T(8,128)})) %all-reduce.33.cloned.1.call-update) | async-done | bytes 131088 | tf_op jit(solution)/shard_map/psum | solution.py:59
  723.5 11.7 %cholesky.55 = f32[128,128]{1,0:T(8,128)S(1)} custom-call(f32[128,128]{1,0:T(8,128)S(1)} %fusion.174), custom_call_target="Cholesky" | custom-call | tf_op jit(solution)/shard_map/jit(cholesky)/cholesky | solution.py:120
  736.4 9.8 %custom-call.9 = f32[1,128,128]{1,2,0:T(8,128)S(1)} custom-call(f32[1,128,128]{2,1,0:T(8,128)S(1)} %fusion.164), custom_call_target="InvertDiagBlocksLowerTriangular" | custom-call | tf_op jit(solution)/shard_map/jit(_cho_solve)/triangular_solve | solution.py:121
  (348 shorter events, 248.0 us)
Async XLA Ops:
  8.4 13.0 %collective-permute-start = (f32[64,8,1]{2,1,0:T(8,128)S(1)}, f32[64,8,1]{2,1,0:T(8,128)S(1)}, u32[]{:S(2)}, u32[]{:S(2)}) collective-permute-start(f32[64,8,1]{2,1,0:T(8,128)S(1)} %broadcast_in_dim.78), channel_id=1, source_target_pairs={{2,0},{4,2},{6,4},{8,6},{10,8},{12,10},{14,12},{0,14},{3,1},{5,3},... | collective-permute-start | bytes 6152 | tf_op jit(solution)/shard_map/ppermute | solution.py:25
  39.1 17.7 %collective-permute-start.10 = (f32[64,1,128]{2,1,0:T(1,128)S(1)}, f32[64,1,128]{2,1,0:T(1,128)S(1)}, u32[]{:S(2)}, u32[]{:S(2)}) collective-permute-start(f32[64,1,128]{2,1,0:T(1,128)S(1)} %get-tuple-element.120), channel_id=1, source_target_pairs={{16,0},{32,16},{48,32},{64,48},{80,64},{96,80},{112,96},{128,112},... | collective-permute-start | bytes 98312 | tf_op jit(solution)/shard_map/ppermute | solution.py:25
  57.3 12.1 %collective-permute-start.13 = (f32[64,1,128]{2,1,0:T(1,128)S(1)}, f32[64,1,128]{2,1,0:T(1,128)S(1)}, u32[]{:S(2)}, u32[]{:S(2)}) collective-permute-start(f32[64,1,128]{2,1,0:T(1,128)S(1)} %get-tuple-element.114), channel_id=1, source_target_pairs={{0,16},{16,32},{32,48},{48,64},{64,80},{80,96},{96,112},{112,128},... | collective-permute-start | bytes 98312 | tf_op jit(solution)/shard_map/ppermute | solution.py:38
  57.4 12.0 %collective-permute-start.14 = (f32[64,1,128]{2,1,0:T(1,128)S(1)}, f32[64,1,128]{2,1,0:T(1,128)S(1)}, u32[]{:S(2)}, u32[]{:S(2)}) collective-permute-start(f32[64,1,128]{2,1,0:T(1,128)S(1)} %get-tuple-element.115), channel_id=1, source_target_pairs={{16,0},{32,16},{48,32},{64,48},{80,64},{96,80},{112,96},{128,112},... | collective-permute-start | bytes 98312 | tf_op jit(solution)/shard_map/ppermute | solution.py:39
  70.6 18.7 %collective-permute-start.18 = (f32[64,1,128]{2,1,0:T(1,128)S(1)}, f32[64,1,128]{2,1,0:T(1,128)S(1)}, u32[]{:S(2)}, u32[]{:S(2)}) collective-permute-start(f32[64,1,128]{2,1,0:T(1,128)S(1)} %get-tuple-element.112), channel_id=1, source_target_pairs={{16,0},{32,16},{48,32},{64,48},{80,64},{96,80},{112,96},{128,112},... | collective-permute-start | bytes 98312 | tf_op jit(solution)/shard_map/ppermute | solution.py:25
  74.4 14.8 %collective-permute-start.19 = (f32[64,1,128]{2,1,0:T(1,128)S(1)}, f32[64,1,128]{2,1,0:T(1,128)S(1)}, u32[]{:S(2)}, u32[]{:S(2)}) collective-permute-start(f32[64,1,128]{2,1,0:T(1,128)S(1)} %get-tuple-element.113), channel_id=1, source_target_pairs={{0,16},{16,32},{32,48},{48,64},{64,80},{80,96},{96,112},{112,128},... | collective-permute-start | bytes 98312 | tf_op jit(solution)/shard_map/ppermute | solution.py:24
  91.1 16.8 %collective-permute-start.20 = (f32[64,8,1]{2,1,0:T(8,128)}, f32[64,8,1]{2,1,0:T(8,128)S(1)}, u32[]{:S(2)}, u32[]{:S(2)}) collective-permute-start(f32[64,8,1]{2,1,0:T(8,128)} %get-tuple-element.108), channel_id=1, source_target_pairs={{0,2},{2,4},{4,6},{6,8},{8,10},{10,12},{12,14},{14,0},{1,3},{3,5},... | collective-permute-start | bytes 6152 | tf_op jit(solution)/shard_map/ppermute | solution.py:38
  91.1 16.8 %collective-permute-start.23 = (f32[64,8,1]{2,1,0:T(8,128)S(1)}, f32[64,8,1]{2,1,0:T(8,128)S(1)}, u32[]{:S(2)}, u32[]{:S(2)}) collective-permute-start(f32[64,8,1]{2,1,0:T(8,128)S(1)} %get-tuple-element.109), channel_id=1, source_target_pairs={{2,0},{4,2},{6,4},{8,6},{10,8},{12,10},{14,12},{0,14},{3,1},{5,3},... | collective-permute-start | bytes 6152 | tf_op jit(solution)/shard_map/ppermute | solution.py:39
  94.3 13.6 %collective-permute-start.21 = (f32[64,1,128]{2,1,0:T(1,128)}, f32[64,1,128]{2,1,0:T(1,128)S(1)}, u32[]{:S(2)}, u32[]{:S(2)}) collective-permute-start(f32[64,1,128]{2,1,0:T(1,128)} %get-tuple-element.106), channel_id=1, source_target_pairs={{0,16},{16,32},{32,48},{48,64},{64,80},{80,96},{96,112},{112,128},... | collective-permute-start | bytes 98312 | tf_op jit(solution)/shard_map/ppermute | solution.py:38
  94.6 13.3 %collective-permute-start.22 = (f32[64,1,128]{2,1,0:T(1,128)}, f32[64,1,128]{2,1,0:T(1,128)}, u32[]{:S(2)}, u32[]{:S(2)}) collective-permute-start(f32[64,1,128]{2,1,0:T(1,128)} %get-tuple-element.107), channel_id=1, source_target_pairs={{16,0},{32,16},{48,32},{64,48},{80,64},{96,80},{112,96},{128,112},... | collective-permute-start | bytes 98312 | tf_op jit(solution)/shard_map/ppermute | solution.py:39
  99.3 78.9 %all-to-all-start = ((f32[4,128,8]{2,0,1:T(4,128)}), f32[4,128,8]{2,0,1:T(4,128)S(1)}, u32[]{:S(2)}, u32[]{:S(2)}) async-start(f32[4,128,8]{2,0,1:T(4,128)} %copy.61), calls=%async_computation | async-start | bytes 524288 | tf_op jit(solution)/shard_map/all_to_all | solution.py:53
  107.8 129.5 %all-reduce.43.cloned.1.call-start = ((), (), s32[]{:S(2)}) async-start(), calls=%async_computation.8 | async-start | bytes 262144 | tf_op jit(solution)/shard_map/psum | solution.py:59
  193.8 94.1 %all-reduce.39.cloned.1.call-start = ((), (), s32[]{:S(2)}) async-start(), calls=%async_computation.6 | async-start | bytes 262144 | tf_op jit(solution)/shard_map/psum | solution.py:59
  237.3 125.3 %all-reduce.35.cloned.1.call-start = ((), (), s32[]{:S(2)}) async-start(), calls=%async_computation.4 | async-start | bytes 262144 | tf_op jit(solution)/shard_map/psum | solution.py:59
  287.9 100.0 %all-gather.3.cloned.1.call-start = ((), (), s32[]{:S(2)}) async-start(), calls=%async_computation.1 | async-start | bytes 1572864 | tf_op jit(solution)/shard_map/all_gather | solution.py:156
  288.5 308.2 %all-reduce.41.cloned.1.call-start = ((), (), s32[]{:S(2)}) async-start(), calls=%async_computation.7 | async-start | bytes 262144 | tf_op jit(solution)/shard_map/psum | solution.py:59
  391.5 12.6 %collective-permute-start.45 = (f32[64,1,128]{2,1,0:T(1,128)S(1)}, f32[64,1,128]{2,1,0:T(1,128)S(1)}, u32[]{:S(2)}, u32[]{:S(2)}) collective-permute-start(f32[64,1,128]{2,1,0:T(1,128)S(1)} %get-tuple-element.82), channel_id=1, source_target_pairs={{0,16},{16,32},{32,48},{48,64},{64,80},{80,96},{96,112},{112,128},... | collective-permute-start | bytes 98312 | tf_op jit(solution)/shard_map/ppermute | solution.py:38
  405.2 17.5 %collective-permute-start.50 = (f32[64,1,128]{2,1,0:T(1,128)S(1)}, f32[64,1,128]{2,1,0:T(1,128)S(1)}, u32[]{:S(2)}, u32[]{:S(2)}) collective-permute-start(f32[64,1,128]{2,1,0:T(1,128)S(1)} %get-tuple-element.80), channel_id=1, source_target_pairs={{16,0},{32,16},{48,32},{64,48},{80,64},{96,80},{112,96},{128,112},... | collective-permute-start | bytes 98312 | tf_op jit(solution)/shard_map/ppermute | solution.py:25
  407.7 15.0 %collective-permute-start.51 = (f32[64,1,128]{2,1,0:T(1,128)S(1)}, f32[64,1,128]{2,1,0:T(1,128)S(1)}, u32[]{:S(2)}, u32[]{:S(2)}) collective-permute-start(f32[64,1,128]{2,1,0:T(1,128)S(1)} %get-tuple-element.81), channel_id=1, source_target_pairs={{0,16},{16,32},{32,48},{48,64},{64,80},{80,96},{96,112},{112,128},... | collective-permute-start | bytes 98312 | tf_op jit(solution)/shard_map/ppermute | solution.py:24
  423.3 14.0 %collective-permute-start.53 = (f32[64,1,128]{2,1,0:T(1,128)S(1)}, f32[64,1,128]{2,1,0:T(1,128)S(1)}, u32[]{:S(2)}, u32[]{:S(2)}) collective-permute-start(f32[64,1,128]{2,1,0:T(1,128)S(1)} %get-tuple-element.74), channel_id=1, source_target_pairs={{0,16},{16,32},{32,48},{48,64},{64,80},{80,96},{96,112},{112,128},... | collective-permute-start | bytes 98312 | tf_op jit(solution)/shard_map/ppermute | solution.py:38
  425.2 12.1 %collective-permute-start.54 = (f32[64,1,128]{2,1,0:T(1,128)S(1)}, f32[64,1,128]{2,1,0:T(1,128)S(1)}, u32[]{:S(2)}, u32[]{:S(2)}) collective-permute-start(f32[64,1,128]{2,1,0:T(1,128)S(1)} %get-tuple-element.75), channel_id=1, source_target_pairs={{16,0},{32,16},{48,32},{64,48},{80,64},{96,80},{112,96},{128,112},... | collective-permute-start | bytes 98312 | tf_op jit(solution)/shard_map/ppermute | solution.py:39
  438.4 17.3 %collective-permute-start.58 = (f32[64,1,128]{2,1,0:T(1,128)S(1)}, f32[64,1,128]{2,1,0:T(1,128)S(1)}, u32[]{:S(2)}, u32[]{:S(2)}) collective-permute-start(f32[64,1,128]{2,1,0:T(1,128)S(1)} %get-tuple-element.72), channel_id=1, source_target_pairs={{16,0},{32,16},{48,32},{64,48},{80,64},{96,80},{112,96},{128,112},... | collective-permute-start | bytes 98312 | tf_op jit(solution)/shard_map/ppermute | solution.py:25
  441.1 14.6 %collective-permute-start.59 = (f32[64,1,128]{2,1,0:T(1,128)S(1)}, f32[64,1,128]{2,1,0:T(1,128)S(1)}, u32[]{:S(2)}, u32[]{:S(2)}) collective-permute-start(f32[64,1,128]{2,1,0:T(1,128)S(1)} %get-tuple-element.73), channel_id=1, source_target_pairs={{0,16},{16,32},{32,48},{48,64},{64,80},{80,96},{96,112},{112,128},... | collective-permute-start | bytes 98312 | tf_op jit(solution)/shard_map/ppermute | solution.py:24
  456.1 13.5 %collective-permute-start.61 = (f32[64,1,128]{2,1,0:T(1,128)S(1)}, f32[64,1,128]{2,1,0:T(1,128)S(1)}, u32[]{:S(2)}, u32[]{:S(2)}) collective-permute-start(f32[64,1,128]{2,1,0:T(1,128)S(1)} %get-tuple-element.66), channel_id=1, source_target_pairs={{0,16},{16,32},{32,48},{48,64},{64,80},{80,96},{96,112},{112,128},... | collective-permute-start | bytes 98312 | tf_op jit(solution)/shard_map/ppermute | solution.py:38
  456.3 13.3 %collective-permute-start.62 = (f32[64,1,128]{2,1,0:T(1,128)S(1)}, f32[64,1,128]{2,1,0:T(1,128)S(1)}, u32[]{:S(2)}, u32[]{:S(2)}) collective-permute-start(f32[64,1,128]{2,1,0:T(1,128)S(1)} %get-tuple-element.67), channel_id=1, source_target_pairs={{16,0},{32,16},{48,32},{64,48},{80,64},{96,80},{112,96},{128,112},... | collective-permute-start | bytes 98312 | tf_op jit(solution)/shard_map/ppermute | solution.py:39
  470.7 15.6 %collective-permute-start.66 = (f32[64,1,128]{2,1,0:T(1,128)S(1)}, f32[64,1,128]{2,1,0:T(1,128)S(1)}, u32[]{:S(2)}, u32[]{:S(2)}) collective-permute-start(f32[64,1,128]{2,1,0:T(1,128)S(1)} %get-tuple-element.64), channel_id=1, source_target_pairs={{16,0},{32,16},{48,32},{64,48},{80,64},{96,80},{112,96},{128,112},... | collective-permute-start | bytes 98312 | tf_op jit(solution)/shard_map/ppermute | solution.py:25
  486.7 12.0 %collective-permute-start.69 = (f32[64,1,128]{2,1,0:T(1,128)S(1)}, f32[64,1,128]{2,1,0:T(1,128)S(1)}, u32[]{:S(2)}, u32[]{:S(2)}) collective-permute-start(f32[64,1,128]{2,1,0:T(1,128)S(1)} %get-tuple-element.58), channel_id=1, source_target_pairs={{0,16},{16,32},{32,48},{48,64},{64,80},{80,96},{96,112},{112,128},... | collective-permute-start | bytes 98312 | tf_op jit(solution)/shard_map/ppermute | solution.py:38
  499.8 16.9 %collective-permute-start.74 = (f32[64,1,128]{2,1,0:T(1,128)S(1)}, f32[64,1,128]{2,1,0:T(1,128)S(1)}, u32[]{:S(2)}, u32[]{:S(2)}) collective-permute-start(f32[64,1,128]{2,1,0:T(1,128)S(1)} %get-tuple-element.56), channel_id=1, source_target_pairs={{16,0},{32,16},{48,32},{64,48},{80,64},{96,80},{112,96},{128,112},... | collective-permute-start | bytes 98312 | tf_op jit(solution)/shard_map/ppermute | solution.py:25
  504.3 12.4 %collective-permute-start.75 = (f32[64,1,128]{2,1,0:T(1,128)S(1)}, f32[64,1,128]{2,1,0:T(1,128)S(1)}, u32[]{:S(2)}, u32[]{:S(2)}) collective-permute-start(f32[64,1,128]{2,1,0:T(1,128)S(1)} %get-tuple-element.57), channel_id=1, source_target_pairs={{0,16},{16,32},{32,48},{48,64},{64,80},{80,96},{96,112},{112,128},... | collective-permute-start | bytes 98312 | tf_op jit(solution)/shard_map/ppermute | solution.py:24
  552.9 94.1 %all-reduce.37.cloned.1.call-start = ((), (), s32[]{:S(2)}) async-start(), calls=%async_computation.5 | async-start | bytes 262144 | tf_op jit(solution)/shard_map/psum | solution.py:59
  596.8 125.0 %all-reduce.33.cloned.1.call-start = ((), (), s32[]{:S(2)}) async-start(), calls=%async_computation.3 | async-start | bytes 262144 | tf_op jit(solution)/shard_map/psum | solution.py:59
  647.0 99.8 %all-gather.5.cloned.1.call-start = ((), (), s32[]{:S(2)}) async-start(), calls=%async_computation.2 | async-start | bytes 1572864 | tf_op jit(solution)/shard_map/all_gather | solution.py:156
  (77 other events, 738.3 us)
Sparse Core Ops, SparseCore 0:
  193.9 43.3 all-reduce.42
  239.8 48.0 all-reduce.38
  290.2 72.3 all-reduce.34
  553.0 43.6 all-reduce.40
  599.0 48.0 all-reduce.36
  649.3 72.3 all-reduce.32
Sparse Core Ops, SparseCore 1:
  290.2 14.7 all-gather.2
  649.5 14.7 all-gather.4
where the time goes:
time: 768 us; the launch traced here: 759 us
  waiting for transfers between devices  443 us (58%)
  starting transfers between devices  194 us (25%)
  other arithmetic  68.4 us (9%)
  local copies, waits for them, and re-layouts  25.4 us (3%)
  between operations  16.6 us (2%)
    psum x6, waiting for transfers between devices, one_axis_at_a_time(): value = lax.psum(value, axis)  336 us
    ppermute x22, starting transfers between devices, padded_2(): after = lax.ppermute(leading, axis, down)  82.6 us
    ppermute x20, starting transfers between devices, with_halo(): lax.ppermute(leading, axis, [(b, a) for a, b in up])  69 us
    ppermute x22, waiting for transfers between devices, padded_2(): before = lax.ppermute(last, axis, up)  48.1 us
    ppermute x20, waiting for transfers between devices, with_halo(): lax.ppermute(last, axis, up)  28.7 us
    ppermute x22, waiting for transfers between devices, padded_2(): after = lax.ppermute(leading, axis, down)  27.1 us
    ppermute x22, starting transfers between devices, padded_2(): before = lax.ppermute(last, axis, up)  25.1 us
    another operation x6, other arithmetic, solve_weights(): factor = jnp.linalg.cholesky(system)  24.7 us
  transfers between devices with their start and end apart: 93, of which 38 were waited for; matrix products, arithmetic and copies ran while one was open for 8% of the time, Pallas kernels for 0%

commit v1 on v0

--- a/solution.py
+++ b/solution.py
@@ -56,7 +56,7 @@
 
 def one_axis_at_a_time(value, axes):
     for axis in axes:
-        value = lax.psum(value, axis)
+        value = jnp.sum(jax.lax.all_gather(value, axis), axis=0)
     return value
 
 

time: 768 us -> 625 us (0.81)
  waiting for transfers between devices: 443 us -> 110 us
  blocking collectives: 4.37 us -> 205 us
    psum x6 -> x0, waiting for transfers between devices: 336 us -> none  [one_axis_at_a_time(): value = lax.psum(value, axis)]
    all_gather x0 -> x12, blocking collectives: none -> 201 us  [one_axis_at_a_time(): value = jnp.sum(jax.lax.all_gather(value, axis), axis=0)]
  transfers between devices with their start and end apart: 93 -> 87, of which waited for: 38 -> 32; matrix products, arithmetic and copies ran while one was open for 8% -> 12% of each run, Pallas kernels for 0% -> 0%
where the time goes in v1:
time: 625 us; the launch traced here: 615 us
  blocking collectives  205 us (33%)
  starting transfers between devices  192 us (31%)
  waiting for transfers between devices  110 us (18%)
  other arithmetic  67.1 us (11%)
  local copies, waits for them, and re-layouts  21.2 us (3%)
  between operations  15.2 us (2%)
    all_gather x12, blocking collectives, one_axis_at_a_time(): value = jnp.sum(jax.lax.all_gather(value, axis), axis=0)  201 us
    ppermute x22, starting transfers between devices, padded_2(): after = lax.ppermute(leading, axis, down)  78.7 us
    ppermute x20, starting transfers between devices, with_halo(): lax.ppermute(leading, axis, [(b, a) for a, b in up])  70.8 us
    ppermute x22, waiting for transfers between devices, padded_2(): before = lax.ppermute(last, axis, up)  49.8 us
    ppermute x22, waiting for transfers between devices, padded_2(): after = lax.ppermute(leading, axis, down)  28.7 us
    ppermute x20, waiting for transfers between devices, with_halo(): lax.ppermute(last, axis, up)  28.5 us
    ppermute x22, starting transfers between devices, padded_2(): before = lax.ppermute(last, axis, up)  28.1 us
    another operation x6, other arithmetic, solve_weights(): factor = jnp.linalg.cholesky(system)  24.9 us
  transfers between devices with their start and end apart: 87, of which 32 were waited for; matrix products, arithmetic and copies ran while one was open for 12% of the time, Pallas kernels for 0%

profile of v1, /device:TPU:2, one launch (start us, length us, event | category | flops | bytes accessed | tf_op | source)
XLA Modules:
  0.0 615.3 jit_solution(10529267531389008290)
XLA Ops:
  7.5 5.9 collective-permute-start
  13.7 4.9 collective-permute-start.2
  38.2 6.0 collective-permute-start.10
  79.3 5.8 collective-permute-done.16
  96.9 8.5 %all-to-all-start = ((f32[4,128,8]{2,0,1:T(4,128)}), f32[4,128,8]{2,0,1:T(4,128)S(1)}, u32[]{:S(2)}, u32[]{:S(2)}) async-start(f32[4,128,8]{2,0,1:T(4,128)} %copy.90), calls=%async_computation | async-start | bytes 524288 | tf_op jit(solution)/shard_map/all_to_all | solution.py:53
  110.3 4.5 collective-permute-start.26
  137.7 5.8 collective-permute-start.34
  146.1 5.4 collective-permute-done.35
  166.7 6.1 collective-permute-start.42
  175.3 5.6 collective-permute-done.43
  188.7 13.1 %all-gather = f32[512,128]{1,0:T(8,128)S(1)} all-gather(f32[128,128]{1,0:T(8,128)S(1)} %fusion.3), channel_id=2, replica_groups=mesh['lat_0'=4,'lat_1'=4,'lon'=8,'ens'=2] {'lat_0'}, dimensions={0}, use_global_device_ids=true | all-gather | bytes 327680 | tf_op jit(solution)/shard_map/all_gather | solution.py:59
  201.8 12.3 %all-gather.1 = f32[512,128]{1,0:T(8,128)S(1)} all-gather(f32[128,128]{1,0:T(8,128)S(1)} %reduce_sum.145), channel_id=3, replica_groups=mesh['lat_0'=4,'lat_1'=4,'lon'=8,'ens'=2] {'lat_1'}, dimensions={0}, use_global_device_ids=true | all-gather | bytes 327680 | tf_op jit(solution)/shard_map/all_gather | solution.py:59
  214.1 25.3 %all-gather.2 = f32[1024,128]{1,0:T(8,128)S(1)} all-gather(f32[128,128]{1,0:T(8,128)S(1)} %reduce_sum.146), channel_id=4, replica_groups=mesh['lat_0'=4,'lat_1'=4,'lon'=8,'ens'=2] {'lon'}, dimensions={0}, use_global_device_ids=true | all-gather | bytes 589824 | tf_op jit(solution)/shard_map/all_gather | solution.py:59
  239.7 11.7 %cholesky.44 = f32[128,128]{1,0:T(8,128)S(1)} custom-call(f32[128,128]{1,0:T(8,128)S(1)} %fusion.178), custom_call_target="Cholesky" | custom-call | tf_op jit(solution)/shard_map/jit(cholesky)/cholesky | solution.py:120
  253.4 12.3 %all-gather.3 = f32[512,128]{1,0:T(8,128)S(1)} all-gather(f32[128,128]{1,0:T(8,128)S(1)} %fusion.2), channel_id=5, replica_groups=mesh['lat_0'=4,'lat_1'=4,'lon'=8,'ens'=2] {'lat_0'}, dimensions={0}, use_global_device_ids=true | all-gather | bytes 327680 | tf_op jit(solution)/shard_map/all_gather | solution.py:59
  265.6 9.8 %custom-call.8 = f32[1,128,128]{1,2,0:T(8,128)S(1)} custom-call(f32[1,128,128]{2,1,0:T(8,128)S(1)} %fusion.163), custom_call_target="InvertDiagBlocksLowerTriangular" | custom-call | tf_op jit(solution)/shard_map/jit(_cho_solve)/triangular_solve | solution.py:121
  275.5 12.3 %all-gather.4 = f32[512,128]{1,0:T(8,128)S(1)} all-gather(f32[128,128]{1,0:T(8,128)S(1)} %reduce_sum.148), channel_id=6, replica_groups=mesh['lat_0'=4,'lat_1'=4,'lon'=8,'ens'=2] {'lat_1'}, dimensions={0}, use_global_device_ids=true | all-gather | bytes 327680 | tf_op jit(solution)/shard_map/all_gather | solution.py:59
  287.7 25.6 %all-gather.5 = f32[1024,128]{1,0:T(8,128)S(1)} all-gather(f32[128,128]{1,0:T(8,128)S(1)} %reduce_sum.149), channel_id=7, replica_groups=mesh['lat_0'=4,'lat_1'=4,'lon'=8,'ens'=2] {'lon'}, dimensions={0}, use_global_device_ids=true | all-gather | bytes 589824 | tf_op jit(solution)/shard_map/all_gather | solution.py:59
  317.6 4.5 collective-permute-start.46
  341.8 6.4 %collective-permute-done.48 = f32[64,8,1]{2,1,0:T(8,128)S(1)} collective-permute-done((f32[64,8,1]{2,1,0:T(8,128)S(1)}, f32[64,8,1]{2,1,0:T(8,128)S(1)}, u32[]{:S(2)}, u32[]{:S(2)}) %collective-permute-start.48) | collective-permute-done | bytes 2080 | tf_op jit(solution)/shard_map/ppermute | solution.py:25
  359.8 5.4 collective-permute-done.52
  410.4 5.2 collective-permute-done.65
  459.5 6.0 collective-permute-start.82
  467.9 5.5 collective-permute-done.83
  480.2 12.4 %all-gather.6 = f32[512,128]{1,0:T(8,128)S(1)} all-gather(f32[128,128]{1,0:T(8,128)S(1)} %fusion.1), channel_id=8, replica_groups=mesh['lat_0'=4,'lat_1'=4,'lon'=8,'ens'=2] {'lat_0'}, dimensions={0}, use_global_device_ids=true | all-gather | bytes 327680 | tf_op jit(solution)/shard_map/all_gather | solution.py:59
  492.6 12.3 %all-gather.7 = f32[512,128]{1,0:T(8,128)S(1)} all-gather(f32[128,128]{1,0:T(8,128)S(1)} %reduce_sum.153), channel_id=9, replica_groups=mesh['lat_0'=4,'lat_1'=4,'lon'=8,'ens'=2] {'lat_1'}, dimensions={0}, use_global_device_ids=true | all-gather | bytes 327680 | tf_op jit(solution)/shard_map/all_gather | solution.py:59
  504.8 25.7 %all-gather.8 = f32[1024,128]{1,0:T(8,128)S(1)} all-gather(f32[128,128]{1,0:T(8,128)S(1)} %reduce_sum.154), channel_id=10, replica_groups=mesh['lat_0'=4,'lat_1'=4,'lon'=8,'ens'=2] {'lon'}, dimensions={0}, use_global_device_ids=true | all-gather | bytes 589824 | tf_op jit(solution)/shard_map/all_gather | solution.py:59
  530.9 11.7 %cholesky.55 = f32[128,128]{1,0:T(8,128)S(1)} custom-call(f32[128,128]{1,0:T(8,128)S(1)} %fusion.174), custom_call_target="Cholesky" | custom-call | tf_op jit(solution)/shard_map/jit(cholesky)/cholesky | solution.py:120
  544.7 12.3 %all-gather.9 = f32[512,128]{1,0:T(8,128)S(1)} all-gather(f32[128,128]{1,0:T(8,128)S(1)} %fusion), channel_id=11, replica_groups=mesh['lat_0'=4,'lat_1'=4,'lon'=8,'ens'=2] {'lat_0'}, dimensions={0}, use_global_device_ids=true | all-gather | bytes 327680 | tf_op jit(solution)/shard_map/all_gather | solution.py:59
  556.9 9.8 %custom-call.9 = f32[1,128,128]{1,2,0:T(8,128)S(1)} custom-call(f32[1,128,128]{2,1,0:T(8,128)S(1)} %fusion.164), custom_call_target="InvertDiagBlocksLowerTriangular" | custom-call | tf_op jit(solution)/shard_map/jit(_cho_solve)/triangular_solve | solution.py:121
  566.8 12.3 %all-gather.10 = f32[512,128]{1,0:T(8,128)S(1)} all-gather(f32[128,128]{1,0:T(8,128)S(1)} %reduce_sum.156), channel_id=12, replica_groups=mesh['lat_0'=4,'lat_1'=4,'lon'=8,'ens'=2] {'lat_1'}, dimensions={0}, use_global_device_ids=true | all-gather | bytes 327680 | tf_op jit(solution)/shard_map/all_gather | solution.py:59
  579.0 25.2 %all-gather.11 = f32[1024,128]{1,0:T(8,128)S(1)} all-gather(f32[128,128]{1,0:T(8,128)S(1)} %reduce_sum.157), channel_id=13, replica_groups=mesh['lat_0'=4,'lat_1'=4,'lon'=8,'ens'=2] {'lon'}, dimensions={0}, use_global_device_ids=true | all-gather | bytes 589824 | tf_op jit(solution)/shard_map/all_gather | solution.py:59
  (352 shorter events, 264.3 us)
Async XLA Ops:
  6.5 307.5 %all-gather.15.cloned.1.call-start = ((), (), s32[]{:S(2)}) async-start(), calls=%async_computation.1 | async-start | bytes 1572864 | tf_op jit(solution)/shard_map/all_gather | solution.py:156
  7.5 13.0 %collective-permute-start = (f32[64,8,1]{2,1,0:T(8,128)S(1)}, f32[64,8,1]{2,1,0:T(8,128)S(1)}, u32[]{:S(2)}, u32[]{:S(2)}) collective-permute-start(f32[64,8,1]{2,1,0:T(8,128)S(1)} %broadcast_in_dim.78), channel_id=1, source_target_pairs={{2,0},{4,2},{6,4},{8,6},{10,8},{12,10},{14,12},{0,14},{3,1},{5,3},... | collective-permute-start | bytes 6152 | tf_op jit(solution)/shard_map/ppermute | solution.py:25
  38.2 17.7 %collective-permute-start.10 = (f32[64,1,128]{2,1,0:T(1,128)S(1)}, f32[64,1,128]{2,1,0:T(1,128)S(1)}, u32[]{:S(2)}, u32[]{:S(2)}) collective-permute-start(f32[64,1,128]{2,1,0:T(1,128)S(1)} %get-tuple-element.108), channel_id=1, source_target_pairs={{16,0},{32,16},{48,32},{64,48},{80,64},{96,80},{112,96},{128,112},... | collective-permute-start | bytes 98312 | tf_op jit(solution)/shard_map/ppermute | solution.py:25
  44.3 11.7 %collective-permute-start.11 = (f32[64,1,128]{2,1,0:T(1,128)S(1)}, f32[64,1,128]{2,1,0:T(1,128)S(1)}, u32[]{:S(2)}, u32[]{:S(2)}) collective-permute-start(f32[64,1,128]{2,1,0:T(1,128)S(1)} %get-tuple-element.109), channel_id=1, source_target_pairs={{0,16},{16,32},{32,48},{48,64},{64,80},{80,96},{96,112},{112,128},... | collective-permute-start | bytes 98312 | tf_op jit(solution)/shard_map/ppermute | solution.py:24
  56.5 12.1 %collective-permute-start.13 = (f32[64,1,128]{2,1,0:T(1,128)S(1)}, f32[64,1,128]{2,1,0:T(1,128)S(1)}, u32[]{:S(2)}, u32[]{:S(2)}) collective-permute-start(f32[64,1,128]{2,1,0:T(1,128)S(1)} %get-tuple-element.102), channel_id=1, source_target_pairs={{0,16},{16,32},{32,48},{48,64},{64,80},{80,96},{96,112},{112,128},... | collective-permute-start | bytes 98312 | tf_op jit(solution)/shard_map/ppermute | solution.py:38
  56.6 12.0 %collective-permute-start.14 = (f32[64,1,128]{2,1,0:T(1,128)S(1)}, f32[64,1,128]{2,1,0:T(1,128)S(1)}, u32[]{:S(2)}, u32[]{:S(2)}) collective-permute-start(f32[64,1,128]{2,1,0:T(1,128)S(1)} %get-tuple-element.103), channel_id=1, source_target_pairs={{16,0},{32,16},{48,32},{64,48},{80,64},{96,80},{112,96},{128,112},... | collective-permute-start | bytes 98312 | tf_op jit(solution)/shard_map/ppermute | solution.py:39
  69.7 17.8 %collective-permute-start.18 = (f32[64,1,128]{2,1,0:T(1,128)S(1)}, f32[64,1,128]{2,1,0:T(1,128)S(1)}, u32[]{:S(2)}, u32[]{:S(2)}) collective-permute-start(f32[64,1,128]{2,1,0:T(1,128)S(1)} %get-tuple-element.100), channel_id=1, source_target_pairs={{16,0},{32,16},{48,32},{64,48},{80,64},{96,80},{112,96},{128,112},... | collective-permute-start | bytes 98312 | tf_op jit(solution)/shard_map/ppermute | solution.py:25
  73.6 13.9 %collective-permute-start.19 = (f32[64,1,128]{2,1,0:T(1,128)S(1)}, f32[64,1,128]{2,1,0:T(1,128)S(1)}, u32[]{:S(2)}, u32[]{:S(2)}) collective-permute-start(f32[64,1,128]{2,1,0:T(1,128)S(1)} %get-tuple-element.101), channel_id=1, source_target_pairs={{0,16},{16,32},{32,48},{48,64},{64,80},{80,96},{96,112},{112,128},... | collective-permute-start | bytes 98312 | tf_op jit(solution)/shard_map/ppermute | solution.py:24
  88.6 16.8 %collective-permute-start.20 = (f32[64,8,1]{2,1,0:T(8,128)S(1)}, f32[64,8,1]{2,1,0:T(8,128)S(1)}, u32[]{:S(2)}, u32[]{:S(2)}) collective-permute-start(f32[64,8,1]{2,1,0:T(8,128)S(1)} %get-tuple-element.96), channel_id=1, source_target_pairs={{0,2},{2,4},{4,6},{6,8},{8,10},{10,12},{12,14},{14,0},{1,3},{3,5},... | collective-permute-start | bytes 6152 | tf_op jit(solution)/shard_map/ppermute | solution.py:38
  88.6 16.8 %collective-permute-start.23 = (f32[64,8,1]{2,1,0:T(8,128)S(1)}, f32[64,8,1]{2,1,0:T(8,128)S(1)}, u32[]{:S(2)}, u32[]{:S(2)}) collective-permute-start(f32[64,8,1]{2,1,0:T(8,128)S(1)} %get-tuple-element.97), channel_id=1, source_target_pairs={{2,0},{4,2},{6,4},{8,6},{10,8},{12,10},{14,12},{0,14},{3,1},{5,3},... | collective-permute-start | bytes 6152 | tf_op jit(solution)/shard_map/ppermute | solution.py:39
  91.9 13.6 %collective-permute-start.21 = (f32[64,1,128]{2,1,0:T(1,128)}, f32[64,1,128]{2,1,0:T(1,128)S(1)}, u32[]{:S(2)}, u32[]{:S(2)}) collective-permute-start(f32[64,1,128]{2,1,0:T(1,128)} %get-tuple-element.94), channel_id=1, source_target_pairs={{0,16},{16,32},{32,48},{48,64},{64,80},{80,96},{96,112},{112,128},... | collective-permute-start | bytes 98312 | tf_op jit(solution)/shard_map/ppermute | solution.py:38
  92.2 13.3 %collective-permute-start.22 = (f32[64,1,128]{2,1,0:T(1,128)}, f32[64,1,128]{2,1,0:T(1,128)}, u32[]{:S(2)}, u32[]{:S(2)}) collective-permute-start(f32[64,1,128]{2,1,0:T(1,128)} %get-tuple-element.95), channel_id=1, source_target_pairs={{16,0},{32,16},{48,32},{64,48},{80,64},{96,80},{112,96},{128,112},... | collective-permute-start | bytes 98312 | tf_op jit(solution)/shard_map/ppermute | solution.py:39
  96.9 78.1 %all-to-all-start = ((f32[4,128,8]{2,0,1:T(4,128)}), f32[4,128,8]{2,0,1:T(4,128)S(1)}, u32[]{:S(2)}, u32[]{:S(2)}) async-start(f32[4,128,8]{2,0,1:T(4,128)} %copy.90), calls=%async_computation | async-start | bytes 524288 | tf_op jit(solution)/shard_map/all_to_all | solution.py:53
  105.4 499.5 %all-gather.17.cloned.1.call-start = ((), (), s32[]{:S(2)}) async-start(), calls=%async_computation.2 | async-start | bytes 1572864 | tf_op jit(solution)/shard_map/all_gather | solution.py:156
  164.0 11.3 %collective-permute-start.40 = (f32[64,8,1]{2,1,0:T(8,128)S(1)}, f32[64,8,1]{2,1,0:T(8,128)S(1)}, u32[]{:S(2)}, u32[]{:S(2)}) collective-permute-start(f32[64,8,1]{2,1,0:T(8,128)S(1)} %get-tuple-element.74), channel_id=1, source_target_pairs={{2,0},{4,2},{6,4},{8,6},{10,8},{12,10},{14,12},{0,14},{3,1},{5,3},... | collective-permute-start | bytes 6152 | tf_op jit(solution)/shard_map/ppermute | solution.py:25
  317.5 15.1 %collective-permute-start.45 = (f32[64,1,128]{2,1,0:T(1,128)S(1)}, f32[64,1,128]{2,1,0:T(1,128)S(1)}, u32[]{:S(2)}, u32[]{:S(2)}) collective-permute-start(f32[64,1,128]{2,1,0:T(1,128)S(1)} %get-tuple-element.70), channel_id=1, source_target_pairs={{0,16},{16,32},{32,48},{48,64},{64,80},{80,96},{96,112},{112,128},... | collective-permute-start | bytes 98312 | tf_op jit(solution)/shard_map/ppermute | solution.py:38
  317.6 15.0 %collective-permute-start.46 = (f32[64,1,128]{2,1,0:T(1,128)S(1)}, f32[64,1,128]{2,1,0:T(1,128)S(1)}, u32[]{:S(2)}, u32[]{:S(2)}) collective-permute-start(f32[64,1,128]{2,1,0:T(1,128)S(1)} %get-tuple-element.71), channel_id=1, source_target_pairs={{16,0},{32,16},{48,32},{64,48},{80,64},{96,80},{112,96},{128,112},... | collective-permute-start | bytes 98312 | tf_op jit(solution)/shard_map/ppermute | solution.py:39
  333.7 17.9 %collective-permute-start.50 = (f32[64,1,128]{2,1,0:T(1,128)S(1)}, f32[64,1,128]{2,1,0:T(1,128)S(1)}, u32[]{:S(2)}, u32[]{:S(2)}) collective-permute-start(f32[64,1,128]{2,1,0:T(1,128)S(1)} %get-tuple-element.68), channel_id=1, source_target_pairs={{16,0},{32,16},{48,32},{64,48},{80,64},{96,80},{112,96},{128,112},... | collective-permute-start | bytes 98312 | tf_op jit(solution)/shard_map/ppermute | solution.py:25
  335.7 16.0 %collective-permute-start.51 = (f32[64,1,128]{2,1,0:T(1,128)S(1)}, f32[64,1,128]{2,1,0:T(1,128)S(1)}, u32[]{:S(2)}, u32[]{:S(2)}) collective-permute-start(f32[64,1,128]{2,1,0:T(1,128)S(1)} %get-tuple-element.69), channel_id=1, source_target_pairs={{0,16},{16,32},{32,48},{48,64},{64,80},{80,96},{96,112},{112,128},... | collective-permute-start | bytes 98312 | tf_op jit(solution)/shard_map/ppermute | solution.py:24
  352.2 13.0 %collective-permute-start.53 = (f32[64,1,128]{2,1,0:T(1,128)S(1)}, f32[64,1,128]{2,1,0:T(1,128)S(1)}, u32[]{:S(2)}, u32[]{:S(2)}) collective-permute-start(f32[64,1,128]{2,1,0:T(1,128)S(1)} %get-tuple-element.62), channel_id=1, source_target_pairs={{0,16},{16,32},{32,48},{48,64},{64,80},{80,96},{96,112},{112,128},... | collective-permute-start | bytes 98312 | tf_op jit(solution)/shard_map/ppermute | solution.py:38
  352.6 12.7 %collective-permute-start.54 = (f32[64,1,128]{2,1,0:T(1,128)S(1)}, f32[64,1,128]{2,1,0:T(1,128)S(1)}, u32[]{:S(2)}, u32[]{:S(2)}) collective-permute-start(f32[64,1,128]{2,1,0:T(1,128)S(1)} %get-tuple-element.63), channel_id=1, source_target_pairs={{16,0},{32,16},{48,32},{64,48},{80,64},{96,80},{112,96},{128,112},... | collective-permute-start | bytes 98312 | tf_op jit(solution)/shard_map/ppermute | solution.py:39
  366.4 16.6 %collective-permute-start.58 = (f32[64,1,128]{2,1,0:T(1,128)S(1)}, f32[64,1,128]{2,1,0:T(1,128)S(1)}, u32[]{:S(2)}, u32[]{:S(2)}) collective-permute-start(f32[64,1,128]{2,1,0:T(1,128)S(1)} %get-tuple-element.60), channel_id=1, source_target_pairs={{16,0},{32,16},{48,32},{64,48},{80,64},{96,80},{112,96},{128,112},... | collective-permute-start | bytes 98312 | tf_op jit(solution)/shard_map/ppermute | solution.py:25
  368.6 14.4 %collective-permute-start.59 = (f32[64,1,128]{2,1,0:T(1,128)S(1)}, f32[64,1,128]{2,1,0:T(1,128)S(1)}, u32[]{:S(2)}, u32[]{:S(2)}) collective-permute-start(f32[64,1,128]{2,1,0:T(1,128)S(1)} %get-tuple-element.61), channel_id=1, source_target_pairs={{0,16},{16,32},{32,48},{48,64},{64,80},{80,96},{96,112},{112,128},... | collective-permute-start | bytes 98312 | tf_op jit(solution)/shard_map/ppermute | solution.py:24
  383.3 12.2 %collective-permute-start.61 = (f32[64,1,128]{2,1,0:T(1,128)S(1)}, f32[64,1,128]{2,1,0:T(1,128)S(1)}, u32[]{:S(2)}, u32[]{:S(2)}) collective-permute-start(f32[64,1,128]{2,1,0:T(1,128)S(1)} %get-tuple-element.54), channel_id=1, source_target_pairs={{0,16},{16,32},{32,48},{48,64},{64,80},{80,96},{96,112},{112,128},... | collective-permute-start | bytes 98312 | tf_op jit(solution)/shard_map/ppermute | solution.py:38
  383.6 11.9 %collective-permute-start.62 = (f32[64,1,128]{2,1,0:T(1,128)S(1)}, f32[64,1,128]{2,1,0:T(1,128)S(1)}, u32[]{:S(2)}, u32[]{:S(2)}) collective-permute-start(f32[64,1,128]{2,1,0:T(1,128)S(1)} %get-tuple-element.55), channel_id=1, source_target_pairs={{16,0},{32,16},{48,32},{64,48},{80,64},{96,80},{112,96},{128,112},... | collective-permute-start | bytes 98312 | tf_op jit(solution)/shard_map/ppermute | solution.py:39
  396.7 18.9 %collective-permute-start.66 = (f32[64,1,128]{2,1,0:T(1,128)S(1)}, f32[64,1,128]{2,1,0:T(1,128)S(1)}, u32[]{:S(2)}, u32[]{:S(2)}) collective-permute-start(f32[64,1,128]{2,1,0:T(1,128)S(1)} %get-tuple-element.52), channel_id=1, source_target_pairs={{16,0},{32,16},{48,32},{64,48},{80,64},{96,80},{112,96},{128,112},... | collective-permute-start | bytes 98312 | tf_op jit(solution)/shard_map/ppermute | solution.py:25
  398.9 16.7 %collective-permute-start.67 = (f32[64,1,128]{2,1,0:T(1,128)S(1)}, f32[64,1,128]{2,1,0:T(1,128)S(1)}, u32[]{:S(2)}, u32[]{:S(2)}) collective-permute-start(f32[64,1,128]{2,1,0:T(1,128)S(1)} %get-tuple-element.53), channel_id=1, source_target_pairs={{0,16},{16,32},{32,48},{48,64},{64,80},{80,96},{96,112},{112,128},... | collective-permute-start | bytes 98312 | tf_op jit(solution)/shard_map/ppermute | solution.py:24
  415.9 12.0 %collective-permute-start.69 = (f32[64,1,128]{2,1,0:T(1,128)S(1)}, f32[64,1,128]{2,1,0:T(1,128)S(1)}, u32[]{:S(2)}, u32[]{:S(2)}) collective-permute-start(f32[64,1,128]{2,1,0:T(1,128)S(1)} %get-tuple-element.46), channel_id=1, source_target_pairs={{0,16},{16,32},{32,48},{48,64},{64,80},{80,96},{96,112},{112,128},... | collective-permute-start | bytes 98312 | tf_op jit(solution)/shard_map/ppermute | solution.py:38
  416.3 11.6 %collective-permute-start.70 = (f32[64,1,128]{2,1,0:T(1,128)S(1)}, f32[64,1,128]{2,1,0:T(1,128)S(1)}, u32[]{:S(2)}, u32[]{:S(2)}) collective-permute-start(f32[64,1,128]{2,1,0:T(1,128)S(1)} %get-tuple-element.47), channel_id=1, source_target_pairs={{16,0},{32,16},{48,32},{64,48},{80,64},{96,80},{112,96},{128,112},... | collective-permute-start | bytes 98312 | tf_op jit(solution)/shard_map/ppermute | solution.py:39
  429.1 16.9 %collective-permute-start.74 = (f32[64,1,128]{2,1,0:T(1,128)S(1)}, f32[64,1,128]{2,1,0:T(1,128)S(1)}, u32[]{:S(2)}, u32[]{:S(2)}) collective-permute-start(f32[64,1,128]{2,1,0:T(1,128)S(1)} %get-tuple-element.44), channel_id=1, source_target_pairs={{16,0},{32,16},{48,32},{64,48},{80,64},{96,80},{112,96},{128,112},... | collective-permute-start | bytes 98312 | tf_op jit(solution)/shard_map/ppermute | solution.py:25
  432.9 13.1 %collective-permute-start.75 = (f32[64,1,128]{2,1,0:T(1,128)S(1)}, f32[64,1,128]{2,1,0:T(1,128)S(1)}, u32[]{:S(2)}, u32[]{:S(2)}) collective-permute-start(f32[64,1,128]{2,1,0:T(1,128)S(1)} %get-tuple-element.45), channel_id=1, source_target_pairs={{0,16},{16,32},{32,48},{48,64},{64,80},{80,96},{96,112},{112,128},... | collective-permute-start | bytes 98312 | tf_op jit(solution)/shard_map/ppermute | solution.py:24
  457.3 10.6 %collective-permute-start.80 = (f32[64,8,1]{2,1,0:T(8,128)S(1)}, f32[64,8,1]{2,1,0:T(8,128)S(1)}, u32[]{:S(2)}, u32[]{:S(2)}) collective-permute-start(f32[64,8,1]{2,1,0:T(8,128)S(1)} %get-tuple-element.34), channel_id=1, source_target_pairs={{2,0},{4,2},{6,4},{8,6},{10,8},{12,10},{14,12},{0,14},{3,1},{5,3},... | collective-permute-start | bytes 6152 | tf_op jit(solution)/shard_map/ppermute | solution.py:25
  (69 other events, 710.0 us)
Sparse Core Ops, SparseCore 0:
  79.4 14.2 all-gather.14
  468.0 15.9 all-gather.16
